TPU v7x, 512 devices: a whole 4x4x16 slice. The times are simulated.
512 devices in a mesh: mem: 16 (over z), sp: 32 (over x, y, core).
Axes of the slice: x: 4, y: 4, z: 16, core: 2. Of those that a mesh axis runs over, the one named last changes fastest.
Arguments:
- ensemble: bfloat16 [256, 131072], P('mem', 'sp'), may hold values from -6 to 6
- predicted: bfloat16 [256, 65536], P('mem', 'sp'), may hold values from -2 to 2
- observed: float32 [65536], P('sp'), may hold values from -6 to 6
- perturbation: bfloat16 [256, 65536], P('mem', 'sp'), may hold values from -6 to 6
- noise_variance: float32 [512], P('sp'), may hold values from 0.25 to 4
- block_lists: int32 [32, 64], P('sp'), may hold values from 0 to 511, as said below
- localization: int32 [1024, 64], P('sp'), may hold values 0 or 1
Outputs:
- increment: float32 [256, 131072], P('mem', 'sp')
Inputs may be any that keep to these rules, and one draw needn't show every extreme that they name: `block_lists`: row t lists the 64 distinct data blocks used by the bricks of index t of sp, in increasing order; block j is held by index j // 16; a row uses 1 to 3 blocks of each holder, exactly 3 of some holder, and every holder gives 3 blocks to some row.
All inputs are finite; a program needn't handle non-finite values. No bound on the sum of `localization` on one device may be relied on, other than what follows from the above.
Results may differ from a plain program's by a relative error of at most 0.0055.
Values may be sent and summed in bfloat16 or wider, within the bound.
No kernel may reach another device: no remote copies, remote signals or barrier semaphores. Data moves between devices by JAX's collectives and lax.ppermute only.
A program may use at most 64 MiB of HBM per device.

v0:
```python
import jax
import jax.numpy as jnp
from jax import lax
from jax.sharding import PartitionSpec as P


def per_device(
    ensemble, predicted, observed, perturbation, noise_variance, block_lists, localization
):
    local_members = ensemble.shape[0]
    members = local_members * lax.axis_size("mem")
    cell_count = ensemble.shape[1]
    brick_count = localization.shape[0]
    brick_size = cell_count // brick_count
    block_count = noise_variance.shape[0]
    block_size = predicted.shape[1] // block_count
    need_count = block_lists.shape[1]
    model_sums, data_sums = lax.psum(
        (
            jnp.sum(ensemble, axis=0, dtype=jnp.float32),
            jnp.sum(predicted, axis=0, dtype=jnp.float32),
        ),
        "mem",
    )
    model_mean = model_sums / members
    data_mean = data_sums / members
    variance = jnp.repeat(noise_variance, block_size)
    innovation = (
        observed[None, :]
        + jnp.sqrt(variance) * perturbation.astype(jnp.float32)
        - predicted.astype(jnp.float32)
    )
    weighted = (innovation / variance).astype(jnp.bfloat16)
    data_anomalies = (predicted.astype(jnp.float32) - data_mean).astype(jnp.bfloat16)
    anomaly_blocks = data_anomalies.reshape(local_members, block_count, block_size)
    portion = lax.all_gather(weighted, "mem", axis=0, tiled=True)
    portion_blocks = portion.reshape(portion.shape[0], block_count, block_size)
    products = jnp.einsum(
        "mjd,njd->jmn", anomaly_blocks, portion_blocks, preferred_element_type=jnp.float32
    )
    products = products.astype(jnp.bfloat16).reshape(block_count, -1)
    row_width = products.shape[1]
    needed = block_lists[0]
    portion = lax.all_gather(products, "sp", axis=0, tiled=True)
    piece_rows = portion.shape[0]
    present = (needed >= 0) & (needed < piece_rows)
    selected = portion[jnp.clip(needed, 0, piece_rows - 1)]
    needed_rows = jnp.where(
        present[:, None], selected, jnp.zeros((need_count, row_width), jnp.bfloat16)
    )
    gain_rows = jnp.dot(
        localization.astype(jnp.bfloat16), needed_rows, preferred_element_type=jnp.float32
    ).astype(jnp.bfloat16)
    gain_blocks = gain_rows.reshape(brick_count, local_members, members)
    model_anomalies = (ensemble.astype(jnp.float32) - model_mean).astype(jnp.bfloat16)
    anomaly_bricks = model_anomalies.reshape(local_members, brick_count, brick_size)
    term_value = jnp.einsum(
        "bmn,mbc->nbc", gain_blocks, anomaly_bricks, preferred_element_type=jnp.float32
    )
    accumulated = lax.psum_scatter(
        term_value.reshape(local_members * lax.axis_size("mem"), cell_count),
        "mem",
        scatter_dimension=0,
        tiled=True,
    )
    return accumulated / (members - 1)


def solution(mesh):
    in_specs = (
        P("mem", "sp"),
        P("mem", "sp"),
        P("sp"),
        P("mem", "sp"),
        P("sp"),
        P("sp", None),
        P("sp", None),
    )
    out_specs = P("mem", "sp")
    return jax.shard_map(
        per_device, mesh=mesh, in_specs=in_specs, out_specs=out_specs, check_vma=False
    )
```

profile of v0, /device:TPU:2, one launch (start us, length us, event | category | flops | bytes accessed | tf_op | source)
XLA Modules:
  0.0 302.7 jit_solution(8834331011151445802)
XLA Ops:
  6.5 0.0 copy-start.2
  6.5 0.0 all-gather.3.cloned.1.call-start
  6.5 0.7 bitcast_sqrt_fusion
  7.3 0.7 broadcast_bitcast_fusion
  8.0 0.9 convert_reduce_fusion.1
  8.9 1.0 convert_reduce_fusion
  9.8 62.0 %all-reduce = (f32[2048]{0:T(1024)S(1)}, f32[4096]{0:T(1024)S(1)}) all-reduce(f32[2048]{0:T(1024)S(1)} %convert_reduce_fusion.1, f32[4096]{0:T(1024)S(1)} %convert_reduce_fusion), channel_id=1, replica_groups=mesh['mem'=16,'sp'=32] {'mem'}, use_global_device_ids=true, to_apply=%region_3.0 | all-reduce | flops 6144 | bytes 49152 | tf_op jit(solution)/shard_map/psum | solution.py:18
  71.8 1.5 fusion.11
  73.4 0.0 all-gather.3.cloned.1.call-update
  73.4 0.0 copy-start.1
  73.4 0.0 all-gather.5.cloned.1.call-start
  73.5 67.2 %all-gather.3.cloned.1.call-done = bf16[256,2048]{1,0:T(8,128)(2,1)} async-done(((bf16[16,2048]{1,0:T(8,128)(2,1)}), bf16[256,2048]{1,0:T(8,128)(2,1)}) %all-gather.3.cloned.1.call-update) | async-done | bytes 1048592 | tf_op jit(solution)/shard_map/all_gather | solution.py:36
  140.7 1.5 copy.19
  142.2 0.0 copy-start
  142.2 0.2 convolution_convert_fusion.1
  142.4 0.7 copy.27
  143.2 0.0 all-gather.5.cloned.1.call-update
  143.2 0.0 reduce-scatter.2.cloned.1.call-start
  143.2 0.0 copy-done.2
  143.3 58.5 %all-gather.5.cloned.1.call-done = bf16[512,4096]{1,0:T(8,128)(2,1)} async-done(((bf16[16,4096]{1,0:T(8,128)(2,1)}), bf16[512,4096]{1,0:T(8,128)(2,1)}) %all-gather.5.cloned.1.call-update) | async-done | bytes 4194320 | tf_op jit(solution)/shard_map/all_gather | solution.py:44
  201.8 4.1 %gather_fusion = bf16[64,4096]{1,0:T(8,128)(2,1)S(1)} fusion(bf16[512,4096]{1,0:T(8,128)(2,1)} %all-gather.5.cloned.1.call-done, s32[1024]{0:T(1024)S(1)} %pad_clamp_fusion), kind=kCustom, calls=%fused_computation | custom fusion | bytes 1048832 | tf_op jit(solution)/shard_map/gather | solution.py:47
  205.9 0.0 copy-done.1
  205.9 0.3 convolution_convert_fusion
  206.2 0.1 copy.28
  206.3 0.0 copy-done
  206.3 2.7 fusion.8
  209.0 5.6 %copy.23 = f32[256,4096]{1,0:T(8,128)} copy(f32[256,4096]{0,1:T(8,128)} %bitcast.32) | data formatting | bytes 8388608 | tf_op jit(solution)/shard_map/reshape | solution.py:61
  214.7 0.0 reduce-scatter.2.cloned.1.call-update
  214.7 79.8 %reduce-scatter.2.cloned.1.call-done = f32[16,4096]{1,0:T(8,128)} async-done(((f32[256,4096]{1,0:T(8,128)}), f32[16,4096]{1,0:T(8,128)}) %reduce-scatter.2.cloned.1.call-update) | async-done | bytes 262160 | tf_op jit(solution)/shard_map/reduce_scatter | solution.py:60
  294.5 1.7 broadcast_multiply_fusion
  (5 shorter events, 0.0 us)
Async XLA Ops:
  6.5 136.7 %copy-start.2 = (s32[1,64]{1,0:T(1,128)S(1)}, s32[1,64]{1,0:T(1,128)}, u32[]{:S(2)}) copy-start(s32[1,64]{1,0:T(1,128)} %param.12) | copy-start | bytes 772
  6.5 134.2 %all-gather.3.cloned.1.call-start = ((), (), s32[]{:S(2)}) async-start(), calls=%async_computation.1 | async-start | bytes 1114112 | tf_op jit(solution)/shard_map/all_gather | solution.py:36
  73.4 132.5 %copy-start.1 = (s32[32,64]{1,0:T(8,128)S(1)}, s32[32,64]{1,0:T(8,128)}, u32[]{:S(2)}) copy-start(s32[32,64]{1,0:T(8,128)} %param.13) | copy-start | bytes 24580
  73.4 128.4 %all-gather.5.cloned.1.call-start = ((), (), s32[]{:S(2)}) async-start(), calls=%async_computation.2 | async-start | bytes 4325376 | tf_op jit(solution)/shard_map/all_gather | solution.py:44
  142.2 64.1 %copy-start = (bf16[16,4096]{1,0:T(8,128)(2,1)S(1)}, bf16[16,4096]{1,0:T(8,128)(2,1)}, u32[]{:S(2)}) copy-start(bf16[16,4096]{1,0:T(8,128)(2,1)} %param.7) | copy-start | bytes 393220
  143.2 151.3 %reduce-scatter.2.cloned.1.call-start = ((), (), s32[]{:S(2)}) async-start(), calls=%async_computation.3 | async-start | bytes 4456448 | tf_op jit(solution)/shard_map/reduce_scatter | solution.py:60
Sparse Core Ops, SparseCore 0:
  73.5 67.1 all-gather.2
  143.8 57.9 all-gather.4
  214.8 79.6 reduce-scatter.1
where the time goes:
time: 303 us
  waiting for transfers between devices  206 us (68%)
  blocking collectives  62 us (20%)
  local copies, waits for them, and re-layouts  13.4 us (4%)
  between operations  13.2 us (4%)
  other arithmetic  5.06 us (2%)
  matrix products  3.25 us (1%)
    reduce_scatter x1, waiting for transfers between devices, per_device(): lax.psum_scatter(term_value.reshape(local_members * lax.axis_size('mem'),...  79.8 us
    all_gather x1, waiting for transfers between devices, per_device(): portion = lax.all_gather(weighted, 'mem', axis=0, tiled=True)  67.2 us
    psum x1, blocking collectives, per_device(): lax.psum((jnp.sum(ensemble, axis=0, dtype=jnp.float32), jnp.sum(predicted...  62 us
    all_gather x1, waiting for transfers between devices, per_device(): portion = lax.all_gather(products, 'sp', axis=0, tiled=True)  58.5 us
  transfers between devices with their start and end apart: 3, of which 3 were waited for; matrix products, arithmetic and copies ran while one was open for 0% of the time, Pallas kernels for 0%

commit v1 on v0

v1 whole, which is shorter than its diff:
```python
import jax
import jax.numpy as jnp
from jax import lax
from jax.sharding import PartitionSpec as P

SLOTS = 3


def per_device(
    ensemble, predicted, observed, perturbation, noise_variance, block_lists, localization
):
    bf16, f32 = jnp.bfloat16, jnp.float32
    mem, sp = lax.axis_size("mem"), lax.axis_size("sp")
    local = ensemble.shape[0]
    members = local * mem
    cells = ensemble.shape[1]
    bricks = localization.shape[0]
    brick = cells // bricks
    blocks = noise_variance.shape[0]
    block = predicted.shape[1] // blocks
    need = block_lists.shape[1]

    whole_ensemble = lax.all_gather(ensemble, "mem", axis=0, tiled=True)

    needed = block_lists[0]
    holder = needed // blocks
    before = jnp.sum(needed[None, :] < (holder * blocks)[:, None], axis=1)
    slot = holder * SLOTS + (jnp.arange(need) - before)
    slot_hot = slot[:, None] == jnp.arange(sp * SLOTS)[None, :]
    asked = jnp.sum(jnp.where(slot_hot, (needed % blocks)[:, None], 0), axis=0)
    asked = jnp.pad(asked.reshape(sp, SLOTS), ((0, 0), (0, 128 - SLOTS)))
    wanted = lax.all_to_all(asked, "sp", split_axis=0, concat_axis=0, tiled=True)
    wanted = wanted[:, :SLOTS].reshape(-1)
    slot_pattern = jnp.dot(
        localization.astype(bf16), slot_hot.astype(bf16), preferred_element_type=f32
    ).astype(bf16)

    cut = (blocks - 1) * block
    last = jnp.broadcast_to(predicted[None, :, cut:], (mem, local, block))
    last = lax.all_to_all(last, "mem", split_axis=0, concat_axis=0, tiled=True)
    first, wanted = lax.optimization_barrier((predicted[:, :cut], wanted))
    first = lax.all_gather(first, "mem", axis=0, tiled=True)
    whole_predicted = jnp.concatenate([first, last.reshape(members, block)], axis=1)

    data_mean = jnp.sum(whole_predicted, axis=0, dtype=f32) / members
    data_anomalies = (whole_predicted.astype(f32) - data_mean).astype(bf16)
    variance = jnp.repeat(noise_variance, block)
    innovation = (
        observed[None, :]
        + jnp.sqrt(variance) * perturbation.astype(f32)
        - predicted.astype(f32)
    )
    weighted = (innovation / variance).astype(bf16)
    products = jnp.einsum(
        "njd,mjd->jnm",
        weighted.reshape(local, blocks, block),
        data_anomalies.reshape(members, blocks, block),
        preferred_element_type=f32,
    ).astype(bf16)
    picked = (wanted[:, None] == jnp.arange(blocks)[None, :]).astype(bf16)
    sent = jnp.einsum("sj,jnm->snm", picked, products, preferred_element_type=f32).astype(bf16)
    sent = sent.reshape(sp, SLOTS * local, members)
    got = lax.all_to_all(sent, "sp", split_axis=0, concat_axis=0, tiled=True)
    got = got.reshape(sp * SLOTS, local, members)
    gains = jnp.einsum("bs,snm->bnm", slot_pattern, got, preferred_element_type=f32).astype(bf16)

    model_mean = jnp.sum(whole_ensemble, axis=0, dtype=f32) / members
    model_anomalies = (whole_ensemble.astype(f32) - model_mean).astype(bf16)
    increment = jnp.einsum(
        "bnm,mbc->nbc",
        gains,
        model_anomalies.reshape(members, bricks, brick),
        preferred_element_type=f32,
    )
    return increment.reshape(local, cells) / (members - 1)


def solution(mesh):
    in_specs = (
        P("mem", "sp"),
        P("mem", "sp"),
        P("sp"),
        P("mem", "sp"),
        P("sp"),
        P("sp", None),
        P("sp", None),
    )
    return jax.shard_map(
        per_device, mesh=mesh, in_specs=in_specs, out_specs=P("mem", "sp"), check_vma=False
    )
```

time: 303 us -> 115 us (0.38)
  the two profiles are of different devices: /device:TPU:2 before, /device:TPU:1 now
where the time goes in v1:
time: 115 us
  blocking collectives  61.8 us (54%)
  starting transfers between devices  23.4 us (20%)
  between operations  13.5 us (12%)
  local copies, waits for them, and re-layouts  5.73 us (5%)
  waiting for transfers between devices  4.72 us (4%)
  other arithmetic  3.88 us (3%)
  matrix products  1.82 us (2%)
    all_gather x1, blocking collectives, per_device(): first = lax.all_gather(first, 'mem', axis=0, tiled=True)  40.6 us
    all_to_all x1, blocking collectives, per_device(): got = lax.all_to_all(sent, 'sp', split_axis=0, concat_axis=0, tiled=True)  21.2 us
    all_to_all x1, starting transfers between devices, per_device(): last = lax.all_to_all(last, 'mem', split_axis=0, concat_axis=0, tiled=True)  13 us
    all_to_all x1, starting transfers between devices, per_device(): lax.all_to_all(asked, 'sp', split_axis=0, concat_axis=0, tiled=True)  10.4 us
    all_to_all x1, waiting for transfers between devices, per_device(): lax.all_to_all(asked, 'sp', split_axis=0, concat_axis=0, tiled=True)  4 us
  transfers between devices with their start and end apart: 3, of which 1 were waited for; matrix products, arithmetic and copies ran while one was open for 7% of the time, Pallas kernels for 0%

profile of v1, /device:TPU:1, one launch (start us, length us, event | category | flops | bytes accessed | tf_op | source)
XLA Modules:
  0.0 114.8 jit_solution(8211245117296514880)
XLA Ops:
  6.5 0.0 all-gather.2.cloned.1.call-start
  6.5 0.7 all-gather.2.cloned.1.call-update
  7.3 0.7 broadcast_multiply_fusion.1
  7.9 0.8 convert_reduce_fusion.2
  8.8 0.1 select_reduce_fusion
  8.9 0.1 reshape.124
  9.0 0.6 pad.4
  9.6 10.4 %all-to-all-start = ((s32[32,1,128]{2,1,0:T(1,128)}), s32[32,1,128]{2,1,0:T(1,128)S(1)}, u32[]{:S(2)}, u32[]{:S(2)}) async-start(s32[32,1,128]{2,1,0:T(1,128)} %bitcast.3), calls=%async_computation | async-start | bytes 32768 | tf_op jit(solution)/shard_map/all_to_all | solution.py:32
  20.0 0.7 bitcast_sqrt_fusion
  20.7 0.7 broadcast_bitcast_fusion
  21.4 0.8 slice.9
  22.3 0.7 slice.11
  23.0 4.0 %all-to-all-done = s32[32,1,128]{2,1,0:T(1,128)S(1)} async-done(((s32[32,1,128]{2,1,0:T(1,128)}), s32[32,1,128]{2,1,0:T(1,128)S(1)}, u32[]{:S(2)}, u32[]{:S(2)}) %all-to-all-start) | async-done | bytes 16416 | tf_op jit(solution)/shard_map/all_to_all | solution.py:32
  27.0 0.6 broadcast_in_dim.19
  27.6 13.0 %all-to-all-start.1 = ((bf16[16,16,128]{2,1,0:T(8,128)(2,1)}), bf16[16,16,128]{2,1,0:T(8,128)(2,1)S(1)}, u32[]{:S(2)}, u32[]{:S(2)}) async-start(bf16[16,16,128]{2,1,0:T(8,128)(2,1)} %broadcast_in_dim.19), calls=%async_computation.1 | async-start | bytes 131072 | tf_op jit(solution)/shard_map/all_to_all | solution.py:40
  40.6 0.1 reshape.125
  40.7 40.6 %all_gather.7 = bf16[256,1920]{1,0:T(8,128)(2,1)S(1)} all-gather(bf16[16,1920]{1,0:T(8,128)(2,1)S(1)} %slice.9), channel_id=1, replica_groups=mesh['mem'=16,'sp'=32] {'mem'}, dimensions={0}, use_global_device_ids=true | all-gather | bytes 1044480 | tf_op jit(solution)/shard_map/all_gather | solution.py:42
  81.4 0.0 all-to-all-done.1
  81.4 0.2 convert_reduce_fusion.1
  81.5 0.0 copy-done.1
  81.5 0.0 copy-done.3
  81.6 0.0 copy-done.4
  81.6 0.4 convolution_convert_fusion.2
  82.0 0.4 convolution_convert_fusion
  82.4 0.4 copy.33
  82.8 21.2 %all_to_all.22 = bf16[32,48,256]{2,1,0:T(8,128)(2,1)S(1)} all-to-all(bf16[32,48,256]{2,1,0:T(8,128)(2,1)S(1)} %bitcast.61), channel_id=1, replica_groups=mesh['mem'=16,'sp'=32] {'sp'}, dimensions={0} | all-to-all | bytes 1572864 | tf_op jit(solution)/shard_map/all_to_all | solution.py:63
  104.0 0.4 convolution_convert_fusion.1
  104.5 0.0 all-gather.2.cloned.1.call-done
  104.5 2.1 %convert_reduce_fusion = f32[4096]{0:T(1024)S(1)} fusion(bf16[256,4096]{1,0:T(8,128)(2,1)} %all-gather.2.cloned.1.call-done), kind=kLoop, calls=%fused_computation.1 | loop fusion | flops 2093056 | bytes 2113536 | tf_op jit(solution)/shard_map/reduce_sum | solution.py:67
  106.6 0.1 copy-done
  106.7 0.6 fusion.9
  107.3 0.7 copy.63
  (9 shorter events, 0.0 us)
Async XLA Ops:
  6.5 75.0 %copy-start.1 = (bf16[16,2048]{1,0:T(8,128)(2,1)S(1)}, bf16[16,2048]{1,0:T(8,128)(2,1)}, u32[]{:S(2)}) copy-start(bf16[16,2048]{1,0:T(8,128)(2,1)} %param.8) | copy-start | bytes 196612
  6.5 75.0 %copy-start.3 = (bf16[16,2048]{1,0:T(8,128)(2,1)S(1)}, bf16[16,2048]{1,0:T(8,128)(2,1)}, u32[]{:S(2)}) copy-start(bf16[16,2048]{1,0:T(8,128)(2,1)} %param.10) | copy-start | bytes 196612
  6.5 75.0 %copy-start.4 = (f32[2048]{0:T(1024)S(1)}, f32[2048]{0:T(1024)}, u32[]{:S(2)}) copy-start(f32[2048]{0:T(1024)} %param.9) | copy-start | bytes 24580
  6.5 97.9 %all-gather.2.cloned.1.call-start = ((), (), s32[]{:S(2)}) async-start(), calls=%async_computation.3 | async-start | bytes 2228224 | tf_op jit(solution)/shard_map/all_gather | solution.py:23
  9.6 17.3 %all-to-all-start = ((s32[32,1,128]{2,1,0:T(1,128)}), s32[32,1,128]{2,1,0:T(1,128)S(1)}, u32[]{:S(2)}, u32[]{:S(2)}) async-start(s32[32,1,128]{2,1,0:T(1,128)} %bitcast.3), calls=%async_computation | async-start | bytes 32768 | tf_op jit(solution)/shard_map/all_to_all | solution.py:32
  27.6 53.8 %all-to-all-start.1 = ((bf16[16,16,128]{2,1,0:T(8,128)(2,1)}), bf16[16,16,128]{2,1,0:T(8,128)(2,1)S(1)}, u32[]{:S(2)}, u32[]{:S(2)}) async-start(bf16[16,16,128]{2,1,0:T(8,128)(2,1)} %broadcast_in_dim.19), calls=%async_computation.1 | async-start | bytes 131072 | tf_op jit(solution)/shard_map/all_to_all | solution.py:40
  82.0 22.1 %copy-start.2 = (s32[32,64]{1,0:T(8,128)S(1)}, s32[32,64]{1,0:T(8,128)}, u32[]{:S(2)}) copy-start(s32[32,64]{1,0:T(8,128)} %param.13) | copy-start | bytes 24580
  104.5 2.2 %copy-start = (bf16[256,4096]{1,0:T(8,128)(2,1)S(1)}, bf16[256,4096]{1,0:T(8,128)(2,1)}, u32[]{:S(2)}) copy-start(bf16[256,4096]{1,0:T(8,128)(2,1)} %all-gather.2.cloned.1.call-done) | copy-start | bytes 6291460
Sparse Core Ops, SparseCore 0:
  9.4 73.4 all-gather.1

commit v2 on v1

v2 whole, which is shorter than its diff:
```python
import jax
import jax.numpy as jnp
from jax import lax
from jax.sharding import PartitionSpec as P

SLOTS = 3
ENSEMBLE_SCALE = 2.0**13
PREDICTED_SCALE = 2.0**14


def per_device(
    ensemble, predicted, observed, perturbation, noise_variance, block_lists, localization
):
    bf16, f16, f32 = jnp.bfloat16, jnp.float16, jnp.float32
    mem, sp = lax.axis_size("mem"), lax.axis_size("sp")
    local = ensemble.shape[0]
    members = local * mem
    cells = ensemble.shape[1]
    bricks = localization.shape[0]
    brick = cells // bricks
    blocks = noise_variance.shape[0]
    data = predicted.shape[1]
    block = data // blocks
    need = block_lists.shape[1]

    needed = block_lists[0]
    holder = needed // blocks
    before = jnp.sum(needed[None, :] < (holder * blocks)[:, None], axis=1)
    slot = holder * SLOTS + (jnp.arange(need) - before)
    slot_hot = slot[:, None] == jnp.arange(sp * SLOTS)[None, :]
    asked = jnp.sum(jnp.where(slot_hot, (needed % blocks)[:, None], 0), axis=0)
    asked = jnp.pad(asked.reshape(sp, SLOTS), ((0, 0), (0, 128 - SLOTS)))
    wanted = lax.all_to_all(asked, "sp", split_axis=0, concat_axis=0, tiled=True)
    wanted = wanted[:, :SLOTS].reshape(-1)
    slot_pattern = jnp.dot(
        localization.astype(bf16), slot_hot.astype(bf16), preferred_element_type=f32
    ).astype(bf16)

    sent = jnp.concatenate(
        [
            (predicted.astype(f32) * PREDICTED_SCALE).astype(f16),
            (ensemble.astype(f32) * ENSEMBLE_SCALE).astype(f16),
        ],
        axis=1,
    )
    whole = lax.all_gather(sent, "mem", axis=0, tiled=True)
    whole_predicted = whole[:, :data].astype(f32)
    whole_ensemble = whole[:, data:].astype(f32)

    data_mean = jnp.sum(whole_predicted, axis=0) / members
    data_anomalies = (whole_predicted - data_mean).astype(bf16)
    variance = jnp.repeat(noise_variance, block)
    innovation = (
        observed[None, :]
        + jnp.sqrt(variance) * perturbation.astype(f32)
        - predicted.astype(f32)
    )
    weighted = (innovation / variance).astype(bf16)
    products = jnp.einsum(
        "njd,mjd->jnm",
        weighted.reshape(local, blocks, block),
        data_anomalies.reshape(members, blocks, block),
        preferred_element_type=f32,
    ).astype(bf16)
    picked = (wanted[:, None] == jnp.arange(blocks)[None, :]).astype(bf16)
    chosen = jnp.einsum("sj,jnm->snm", picked, products, preferred_element_type=f32).astype(bf16)
    chosen = chosen.reshape(sp, SLOTS * local, members)
    got = lax.all_to_all(chosen, "sp", split_axis=0, concat_axis=0, tiled=True)
    got = got.reshape(sp * SLOTS, local, members)
    gains = jnp.einsum("bs,snm->bnm", slot_pattern, got, preferred_element_type=f32).astype(bf16)

    model_mean = jnp.sum(whole_ensemble, axis=0) / members
    model_anomalies = (whole_ensemble - model_mean).astype(bf16)
    increment = jnp.einsum(
        "bnm,mbc->nbc",
        gains,
        model_anomalies.reshape(members, bricks, brick),
        preferred_element_type=f32,
    )
    return increment.reshape(local, cells) / ((members - 1) * (ENSEMBLE_SCALE * PREDICTED_SCALE))


def solution(mesh):
    in_specs = (
        P("mem", "sp"),
        P("mem", "sp"),
        P("sp"),
        P("mem", "sp"),
        P("sp"),
        P("sp", None),
        P("sp", None),
    )
    return jax.shard_map(
        per_device, mesh=mesh, in_specs=in_specs, out_specs=P("mem", "sp"), check_vma=False
    )
```

time: 115 us -> 101 us (0.88)
  between operations: 13.5 us -> 0.1 us
  blocking collectives: 61.8 us -> 50.7 us
  waiting for transfers between devices: 4.72 us -> 14 us
  local copies, waits for them, and re-layouts: 5.73 us -> 4.36 us
    all_to_all x1 -> x0, blocking collectives: 21.2 us -> none  [per_device(): got = lax.all_to_all(sent, 'sp', split_axis=0, concat_axis=0, tiled=True)]
    all_to_all x1, waiting for transfers between devices: 0.01 us -> 14 us  [per_device(): got = lax.all_to_all(chosen, 'sp', split_axis=0, concat_axis=0, tiled=True)]
    all_gather x1, blocking collectives: 40.6 us -> 50.7 us  [per_device(): whole = lax.all_gather(sent, 'mem', axis=0, tiled=True)]
    all_to_all x1, waiting for transfers between devices: 4 us -> 0.01 us  [per_device(): lax.all_to_all(asked, 'sp', split_axis=0, concat_axis=0, tiled=True)]
    reduce_sum x2, other arithmetic: 2.26 us -> 0.48 us  [the longest x1 0.31 us: per_device(): model_mean = jnp.sum(whole_ensemble, axis=0) / members]
    slice x2 -> x0, local copies, waits for them, and re-layouts: 1.52 us -> none  [the longest x1 0.83 us: per_device(): first, wanted = lax.optimization_barrier((predicted[:, :cut], wanted))]
  transfers between devices with their start and end apart: 3 -> 2, of which waited for: 1 -> 1; matrix products, arithmetic and copies ran while one was open for 7% -> 4% of each run, Pallas kernels for 0% -> 0%
where the time goes in v2:
time: 101 us; the launch traced here: 100 us
  blocking collectives  50.7 us (50%)
  starting transfers between devices  24.2 us (24%)
  waiting for transfers between devices  14 us (14%)
  local copies, waits for them, and re-layouts  4.36 us (4%)
  other arithmetic  4 us (4%)
  matrix products  2.93 us (3%)
    all_gather x1, blocking collectives, per_device(): whole = lax.all_gather(sent, 'mem', axis=0, tiled=True)  50.7 us
    all_to_all x1, waiting for transfers between devices, per_device(): got = lax.all_to_all(chosen, 'sp', split_axis=0, concat_axis=0, tiled=True)  14 us
    all_to_all x1, starting transfers between devices, per_device(): got = lax.all_to_all(chosen, 'sp', split_axis=0, concat_axis=0, tiled=True)  13.9 us
    all_to_all x1, starting transfers between devices, per_device(): lax.all_to_all(asked, 'sp', split_axis=0, concat_axis=0, tiled=True)  10.4 us
  transfers between devices with their start and end apart: 2, of which 1 were waited for; matrix products, arithmetic and copies ran while one was open for 4% of the time, Pallas kernels for 0%

profile of v2, /device:TPU:1, one launch (start us, length us, event | category | flops | bytes accessed | tf_op | source)
XLA Modules:
  0.0 100.3 jit_solution(8255561236363733523)
XLA Ops:
  0.0 0.7 broadcast_multiply_fusion.2
  0.7 0.8 convert_reduce_fusion.2
  1.5 0.1 select_reduce_fusion
  1.6 0.1 reshape.108
  1.7 0.6 pad.4
  2.3 10.4 %all-to-all-start = ((s32[32,1,128]{2,1,0:T(1,128)}), s32[32,1,128]{2,1,0:T(1,128)S(1)}, u32[]{:S(2)}, u32[]{:S(2)}) async-start(s32[32,1,128]{2,1,0:T(1,128)} %bitcast.3), calls=%async_computation | async-start | bytes 32768 | tf_op jit(solution)/shard_map/all_to_all | solution.py:33
  12.7 0.7 bitcast_sqrt_fusion
  13.4 0.7 broadcast_bitcast_fusion
  14.2 0.9 multiply_convert_fusion
  15.1 0.9 fusion.24
  16.0 0.1 pad_maximum_fusion
  16.1 50.7 %all-gather.1 = f16[256,6144]{1,0:T(8,128)(2,1)S(1)} all-gather(f16[16,6144]{1,0:T(8,128)(2,1)S(1)} %pad_maximum_fusion), channel_id=1, replica_groups=mesh['mem'=16,'sp'=32] {'mem'}, dimensions={0}, use_global_device_ids=true | all-gather | bytes 3342336 | tf_op jit(solution)/shard_map/all_gather | solution.py:46
  66.8 0.2 convert_reduce_fusion.1
  67.0 0.4 convolution_convert_fusion.2
  67.3 0.0 copy-start
  67.3 0.0 all-to-all-done
  67.4 0.1 eq.33
  67.5 0.4 convolution_convert_fusion
  67.9 1.3 %copy.33 = bf16[96,16,256]{2,1,0:T(8,128)(2,1)} copy(bf16[96,16,256]{2,0,1:T(8,128)(2,1)S(1)} %convolution_convert_fusion) | data formatting | bytes 1572864 | tf_op jit(solution)/shard_map/convert_element_type | solution.py:66
  69.2 13.9 %all-to-all-start.1 = ((bf16[32,48,256]{2,1,0:T(8,128)(2,1)}), bf16[32,48,256]{2,1,0:T(8,128)(2,1)}, u32[]{:S(2)}, u32[]{:S(2)}) async-start(bf16[32,48,256]{2,1,0:T(8,128)(2,1)} %bitcast.54), calls=%async_computation.1 | async-start | bytes 1572864 | tf_op jit(solution)/shard_map/all_to_all | solution.py:68
  83.1 0.3 convert_reduce_fusion
  83.4 14.0 %all-to-all-done.1 = bf16[32,48,256]{2,1,0:T(8,128)(2,1)} async-done(((bf16[32,48,256]{2,1,0:T(8,128)(2,1)}), bf16[32,48,256]{2,1,0:T(8,128)(2,1)}, u32[]{:S(2)}, u32[]{:S(2)}) %all-to-all-start.1) | async-done | bytes 786464 | tf_op jit(solution)/shard_map/all_to_all | solution.py:68
  97.4 0.0 copy-done
  97.4 1.6 %convolution_convert_fusion.1 = bf16[32,16,256]{2,0,1:T(8,128)(2,1)S(1)} fusion(bf16[96,16,256]{2,1,0:T(8,128)(2,1)} %bitcast.8, s32[64]{0:T(128)S(1)} %subtract_add_fusion, s32[32,64]{1,0:T(8,128)S(1)} %copy-done), kind=kOutput, calls=%fused_computation.11 | convolution fusion | flops 25701376 | bytes 1057024 | tf_op jit(solution)/shard_map/bs,snm->bnm/dot_general | solution.py:70
  99.0 0.6 fusion.9
  99.5 0.7 copy.65
  (3 shorter events, 0.0 us)
Async XLA Ops:
  2.3 65.0 %all-to-all-start = ((s32[32,1,128]{2,1,0:T(1,128)}), s32[32,1,128]{2,1,0:T(1,128)S(1)}, u32[]{:S(2)}, u32[]{:S(2)}) async-start(s32[32,1,128]{2,1,0:T(1,128)} %bitcast.3), calls=%async_computation | async-start | bytes 32768 | tf_op jit(solution)/shard_map/all_to_all | solution.py:33
  67.3 30.0 %copy-start = (s32[32,64]{1,0:T(8,128)S(1)}, s32[32,64]{1,0:T(8,128)}, u32[]{:S(2)}) copy-start(s32[32,64]{1,0:T(8,128)} %param.13) | copy-start | bytes 24580
  69.2 28.2 %all-to-all-start.1 = ((bf16[32,48,256]{2,1,0:T(8,128)(2,1)}), bf16[32,48,256]{2,1,0:T(8,128)(2,1)}, u32[]{:S(2)}, u32[]{:S(2)}) async-start(bf16[32,48,256]{2,1,0:T(8,128)(2,1)} %bitcast.54), calls=%async_computation.1 | async-start | bytes 1572864 | tf_op jit(solution)/shard_map/all_to_all | solution.py:68

commit v3 on v2

v3 whole, which is shorter than its diff:
```python
import jax
import jax.numpy as jnp
from jax import lax
from jax.experimental import pallas as pl
from jax.experimental.pallas import tpu as pltpu
from jax.sharding import PartitionSpec as P

SLOTS = 3
SCALE = 2.0**13


def prepare(
    predicted_ref, observed_ref, perturbation_ref, variance_ref, lists_ref, localization_ref,
    weighted_ref, asked_ref, pattern_ref,
):
    bf16, f32 = jnp.bfloat16, jnp.float32
    blocks = variance_ref.shape[1]
    block = predicted_ref.shape[1] // blocks
    for j in range(blocks):
        cut = slice(j * block, (j + 1) * block)
        variance = variance_ref[0, j]
        spread = jnp.full((1, block), variance, f32)
        innovation = (
            observed_ref[:, cut]
            + jnp.sqrt(spread) * perturbation_ref[:, cut].astype(f32)
            - predicted_ref[:, cut].astype(f32)
        )
        weighted_ref[:, cut] = (innovation / spread).astype(bf16)

    need = lists_ref.shape[1]
    holders, lanes = asked_ref.shape
    across = lists_ref[...]
    row = lax.broadcasted_iota(jnp.int32, (need, need), 0)
    column = lax.broadcasted_iota(jnp.int32, (need, need), 1)
    down = jnp.sum(jnp.where(row == column, across, 0), axis=1, keepdims=True)
    holder = lax.div(down, blocks)
    before = jnp.sum((across < holder * blocks).astype(jnp.int32), axis=1, keepdims=True)
    rank = lax.broadcasted_iota(jnp.int32, (need, 1), 0) - before
    lane = lax.broadcasted_iota(jnp.int32, (need, lanes), 1)
    ranked = jnp.where(lane == rank, down - holder * blocks, 0).astype(f32).astype(bf16)
    held = lax.div(across, blocks) == lax.broadcasted_iota(jnp.int32, (holders, need), 0)
    held = held.astype(f32).astype(bf16)
    asked = jnp.dot(held, ranked, preferred_element_type=f32)
    asked_ref[...] = asked.astype(jnp.int32)
    slot_hot = (lane == holder * SLOTS + rank).astype(f32).astype(bf16)
    uses = localization_ref[...].astype(f32).astype(bf16)
    pattern_ref[...] = jnp.dot(uses, slot_hot, preferred_element_type=f32).astype(bf16)


def per_device(
    ensemble, predicted, observed, perturbation, noise_variance, block_lists, localization
):
    bf16, f16, f32 = jnp.bfloat16, jnp.float16, jnp.float32
    mem, sp = lax.axis_size("mem"), lax.axis_size("sp")
    local = ensemble.shape[0]
    members = local * mem
    cells = ensemble.shape[1]
    bricks = localization.shape[0]
    brick = cells // bricks
    blocks = noise_variance.shape[0]
    data = predicted.shape[1]
    block = data // blocks
    slots = sp * SLOTS

    vmem = pl.BlockSpec(memory_space=pltpu.VMEM)
    weighted, asked, pattern = pl.pallas_call(
        prepare,
        out_shape=(
            jax.ShapeDtypeStruct((local, data), bf16),
            jax.ShapeDtypeStruct((sp, 128), jnp.int32),
            jax.ShapeDtypeStruct((bricks, 128), bf16),
        ),
        in_specs=[vmem, vmem, vmem, pl.BlockSpec(memory_space=pltpu.SMEM), vmem, vmem],
        out_specs=(vmem, vmem, vmem),
    )(
        predicted,
        observed.reshape(1, data),
        perturbation,
        noise_variance.reshape(1, blocks),
        block_lists,
        localization,
    )
    wanted = lax.all_to_all(asked, "sp", split_axis=0, concat_axis=0, tiled=True)
    wanted = wanted[:, :SLOTS].reshape(-1)

    sent = jnp.concatenate([predicted, ensemble], axis=1).astype(f32)
    sent = (sent * SCALE).astype(f16)
    whole = lax.all_gather(sent, "mem", axis=0, tiled=True)
    whole_predicted = whole[:, :data].astype(f32)
    whole_ensemble = whole[:, data:].astype(f32)

    data_mean = jnp.sum(whole_predicted, axis=0) / members
    data_anomalies = (whole_predicted - data_mean).astype(bf16)
    products = jnp.einsum(
        "njd,mjd->jnm",
        weighted.reshape(local, blocks, block),
        data_anomalies.reshape(members, blocks, block),
        preferred_element_type=f32,
    ).astype(bf16)
    picked = (wanted[:, None] == jnp.arange(blocks)[None, :]).astype(bf16)
    chosen = jnp.einsum("sj,jnm->snm", picked, products, preferred_element_type=f32).astype(bf16)
    chosen = chosen.reshape(sp, SLOTS * local, members)
    model_mean = jnp.sum(whole_ensemble, axis=0) / members
    chosen, model_mean, pattern = lax.optimization_barrier((chosen, model_mean, pattern))
    got = lax.all_to_all(chosen, "sp", split_axis=0, concat_axis=0, tiled=True)
    got = got.reshape(slots, local, members)
    gains = jnp.einsum(
        "bs,snm->bnm", pattern[:, :slots], got, preferred_element_type=f32
    ).astype(bf16)

    model_anomalies = (whole_ensemble - model_mean).astype(bf16)
    increment = jnp.einsum(
        "bnm,mbc->nbc",
        gains,
        model_anomalies.reshape(members, bricks, brick),
        preferred_element_type=f32,
    )
    return increment.reshape(local, cells) / ((members - 1) * SCALE**2)


def solution(mesh):
    in_specs = (
        P("mem", "sp"),
        P("mem", "sp"),
        P("sp"),
        P("mem", "sp"),
        P("sp"),
        P("sp", None),
        P("sp", None),
    )
    return jax.shard_map(
        per_device, mesh=mesh, in_specs=in_specs, out_specs=P("mem", "sp"), check_vma=False
    )
```

time: 101 us -> 95.7 us (0.948)
  blocking collectives: 50.7 us -> 78.6 us
  waiting for transfers between devices: 14 us -> 0.02 us
  starting transfers between devices: 24.2 us -> 10.4 us
  local copies, waits for them, and re-layouts: 4.36 us -> 1.28 us
  other arithmetic: 4 us -> 1.44 us
  Pallas kernels: 0 us -> 1.82 us
  matrix products: 2.93 us -> 1.75 us
    all_to_all x0 -> x1, blocking collectives: none -> 27.8 us  [per_device(): got = lax.all_to_all(chosen, 'sp', split_axis=0, concat_axis=0, tiled=True)]
    all_to_all x1 -> x0, waiting for transfers between devices: 14 us -> none  [per_device(): got = lax.all_to_all(chosen, 'sp', split_axis=0, concat_axis=0, tiled=True)]
    all_to_all x1 -> x0, starting transfers between devices: 13.9 us -> none  [per_device(): got = lax.all_to_all(chosen, 'sp', split_axis=0, concat_axis=0, tiled=True)]
    pallas_call x0 -> x1, Pallas kernels: none -> 1.82 us  [per_device(): pl.pallas_call(prepare, out_shape=(jax.ShapeDtypeStruct((local, data), bf...]
    dot_general x1, matrix products: 1.58 us -> 0.4 us  [per_device(): jnp.einsum('bs,snm->bnm', pattern[:, :slots], got, preferred_element_type...]
  transfers between devices with their start and end apart: 2 -> 1, of which waited for: 1 -> 0; matrix products, arithmetic and copies ran while one was open for 4% -> 2% of each run, Pallas kernels for 0% -> 0%
where the time goes in v3:
time: 95.7 us; the launch traced here: 95.4 us
  blocking collectives  78.6 us (82%)
  starting transfers between devices  10.4 us (11%)
  Pallas kernels  1.82 us (2%)
  matrix products  1.75 us (2%)
  other arithmetic  1.44 us (2%)
  local copies, waits for them, and re-layouts  1.28 us (1%)
    all_gather x1, blocking collectives, per_device(): whole = lax.all_gather(sent, 'mem', axis=0, tiled=True)  50.8 us
    all_to_all x1, blocking collectives, per_device(): got = lax.all_to_all(chosen, 'sp', split_axis=0, concat_axis=0, tiled=True)  27.8 us
    all_to_all x1, starting transfers between devices, per_device(): lax.all_to_all(asked, 'sp', split_axis=0, concat_axis=0, tiled=True)  10.4 us
  transfers between devices with their start and end apart: 1, of which 0 were waited for; matrix products, arithmetic and copies ran while one was open for 2% of the time, Pallas kernels for 0%

profile of v3, /device:TPU:1, one launch (start us, length us, event | category | flops | bytes accessed | tf_op | source)
XLA Modules:
  0.0 95.4 jit_solution(12757024666546144041)
XLA Ops:
  0.0 1.8 %shard_map.73 = (bf16[16,2048]{1,0:T(8,128)(2,1)}, s32[32,128]{1,0:T(8,128)}, bf16[32,128]{1,0:T(8,128)(2,1)}) custom-call(bf16[16,2048]{1,0:T(8,128)(2,1)} %predicted_ref.1, f32[1,2048]{1,0:T(1,128)} %bitcast.50, bf16[16,2048]{1,0:T(8,128)(2,1)} %perturbation_ref.1, f32[1,16]{1,0:T(1,128)} %bitcast.51, s32[1,64]{1,0:T(1,128)} %lists_ref.1, ...), custom_call_target="tpu_custom_call" | custom-call | tf_op jit(solution)/shard_map/pallas_call | solution.py:66
  1.8 10.4 %all-to-all-start = ((s32[32,1,128]{2,1,0:T(1,128)}), s32[32,1,128]{2,1,0:T(1,128)S(1)}, u32[]{:S(2)}, u32[]{:S(2)}) async-start(s32[32,1,128]{2,1,0:T(1,128)} %bitcast.49), calls=%async_computation | async-start | bytes 32768 | tf_op jit(solution)/shard_map/all_to_all | solution.py:83
  12.2 1.0 %multiply_convert_fusion = f16[16,6144]{1,0:T(8,128)(2,1)S(1)} fusion(bf16[16,4096]{1,0:T(8,128)(2,1)} %param.7, bf16[16,2048]{1,0:T(8,128)(2,1)} %predicted_ref.1), kind=kLoop, calls=%fused_computation.19 | loop fusion | flops 589824 | bytes 393216 | tf_op jit(solution)/shard_map/convert_element_type | solution.py:87
  13.2 0.0 copy-start.1
  13.2 50.8 %all-gather.1 = f16[256,6144]{1,0:T(8,128)(2,1)S(1)} all-gather(f16[16,6144]{1,0:T(8,128)(2,1)S(1)} %multiply_convert_fusion), channel_id=1, replica_groups=mesh['mem'=16,'sp'=32] {'mem'}, dimensions={0}, use_global_device_ids=true | all-gather | bytes 3342336 | tf_op jit(solution)/shard_map/all_gather | solution.py:88
  64.0 0.2 convert_reduce_fusion.1
  64.1 0.3 convert_reduce_fusion
  64.5 0.0 copy-start
  64.5 0.0 copy-done.1
  64.5 0.4 convolution_convert_fusion.2
  64.9 0.0 all-to-all-done
  64.9 0.1 eq.15
  65.0 0.4 convolution_convert_fusion
  65.4 0.4 copy.24
  65.9 27.8 %all_to_all.17 = bf16[32,48,256]{2,1,0:T(8,128)(2,1)S(1)} all-to-all(bf16[32,48,256]{2,1,0:T(8,128)(2,1)S(1)} %bitcast.46), channel_id=1, replica_groups=mesh['mem'=16,'sp'=32] {'sp'}, dimensions={0} | all-to-all | bytes 1572864 | tf_op jit(solution)/shard_map/all_to_all | solution.py:105
  93.7 0.0 copy-done
  93.7 0.4 convolution_convert_fusion.1
  94.1 0.6 fusion.9
  94.7 0.7 copy.56
  (2 shorter events, 0.0 us)
Async XLA Ops:
  1.8 63.1 %all-to-all-start = ((s32[32,1,128]{2,1,0:T(1,128)}), s32[32,1,128]{2,1,0:T(1,128)S(1)}, u32[]{:S(2)}, u32[]{:S(2)}) async-start(s32[32,1,128]{2,1,0:T(1,128)} %bitcast.49), calls=%async_computation | async-start | bytes 32768 | tf_op jit(solution)/shard_map/all_to_all | solution.py:83
  13.2 51.3 %copy-start.1 = (bf16[16,2048]{1,0:T(8,128)(2,1)S(1)}, bf16[16,2048]{1,0:T(8,128)(2,1)}, u32[]{:S(2)}) copy-start(bf16[16,2048]{1,0:T(8,128)(2,1)} %get-tuple-element.12) | copy-start | bytes 196612
  64.5 29.2 %copy-start = (bf16[32,128]{1,0:T(8,128)(2,1)S(1)}, bf16[32,128]{1,0:T(8,128)(2,1)}, u32[]{:S(2)}) copy-start(bf16[32,128]{1,0:T(8,128)(2,1)} %get-tuple-element.15) | copy-start | bytes 24580

commit v4 on v3

v4 whole, which is shorter than its diff:
```python
import jax
import jax.numpy as jnp
from jax import lax
from jax.experimental import pallas as pl
from jax.experimental.pallas import tpu as pltpu
from jax.sharding import PartitionSpec as P

SCALE = 2.0**13


def prepare(
    predicted_ref, observed_ref, perturbation_ref, variance_ref, lists_ref, localization_ref,
    weighted_ref, pattern_ref,
):
    bf16, f32 = jnp.bfloat16, jnp.float32
    blocks = variance_ref.shape[1]
    block = predicted_ref.shape[1] // blocks
    for j in range(blocks):
        cut = slice(j * block, (j + 1) * block)
        spread = jnp.full((1, block), variance_ref[0, j], f32)
        innovation = (
            observed_ref[:, cut]
            + jnp.sqrt(spread) * perturbation_ref[:, cut].astype(f32)
            - predicted_ref[:, cut].astype(f32)
        )
        weighted_ref[:, cut] = (innovation / spread).astype(bf16)

    need = lists_ref.shape[1]
    row = lax.broadcasted_iota(jnp.int32, (need, need), 0)
    column = lax.broadcasted_iota(jnp.int32, (need, need), 1)
    down = jnp.sum(jnp.where(row == column, lists_ref[...], 0), axis=1, keepdims=True)
    lane = lax.broadcasted_iota(jnp.int32, (need, pattern_ref.shape[1]), 1)
    hot = (lane == down).astype(f32).astype(bf16)
    uses = localization_ref[...].astype(f32).astype(bf16)
    pattern_ref[...] = jnp.dot(uses, hot, preferred_element_type=f32).astype(bf16)


def per_device(
    ensemble, predicted, observed, perturbation, noise_variance, block_lists, localization
):
    bf16, f16, f32 = jnp.bfloat16, jnp.float16, jnp.float32
    mem, sp = lax.axis_size("mem"), lax.axis_size("sp")
    local = ensemble.shape[0]
    members = local * mem
    cells = ensemble.shape[1]
    bricks = localization.shape[0]
    brick = cells // bricks
    blocks = noise_variance.shape[0]
    data = predicted.shape[1]
    block = data // blocks

    vmem = pl.BlockSpec(memory_space=pltpu.VMEM)
    weighted, pattern = pl.pallas_call(
        prepare,
        out_shape=(
            jax.ShapeDtypeStruct((local, data), bf16),
            jax.ShapeDtypeStruct((bricks, blocks * sp), bf16),
        ),
        in_specs=[vmem, vmem, vmem, pl.BlockSpec(memory_space=pltpu.SMEM), vmem, vmem],
        out_specs=(vmem, vmem),
    )(
        predicted,
        observed.reshape(1, data),
        perturbation,
        noise_variance.reshape(1, blocks),
        block_lists,
        localization,
    )
    sent = jnp.concatenate([predicted, ensemble], axis=1).astype(f32)
    sent = (sent * SCALE).astype(f16)
    whole = lax.all_gather(sent, "mem", axis=0, tiled=True)
    whole_predicted = whole[:, :data].astype(f32)
    whole_ensemble = whole[:, data:].astype(f32)

    data_mean = jnp.sum(whole_predicted, axis=0) / members
    data_anomalies = (whole_predicted - data_mean).astype(bf16)
    products = jnp.einsum(
        "njd,mjd->jnm",
        weighted.reshape(local, blocks, block),
        data_anomalies.reshape(members, blocks, block),
        preferred_element_type=f32,
    )
    products = (products * (1 / SCALE)).astype(bf16).astype(f16)
    every = lax.all_gather(products, "sp", axis=0, tiled=True)
    gains = jnp.einsum(
        "bj,jnm->bnm", pattern, every.astype(bf16), preferred_element_type=f32
    ).astype(bf16)

    model_mean = jnp.sum(whole_ensemble, axis=0) / members
    model_anomalies = (whole_ensemble - model_mean).astype(bf16)
    increment = jnp.einsum(
        "bnm,mbc->nbc",
        gains,
        model_anomalies.reshape(members, bricks, brick),
        preferred_element_type=f32,
    )
    return increment.reshape(local, cells) / ((members - 1) * SCALE)


def solution(mesh):
    in_specs = (
        P("mem", "sp"),
        P("mem", "sp"),
        P("sp"),
        P("mem", "sp"),
        P("sp"),
        P("sp", None),
        P("sp", None),
    )
    return jax.shard_map(
        per_device, mesh=mesh, in_specs=in_specs, out_specs=P("mem", "sp"), check_vma=False
    )
```

time: 95.7 us -> 96.3 us (level)
  starting transfers between devices: 10.4 us -> 0 us
  blocking collectives: 78.6 us -> 88.9 us
  matrix products: 1.75 us -> 3.29 us
    all_gather x0 -> x1, blocking collectives: none -> 35.6 us  [per_device(): every = lax.all_gather(products, 'sp', axis=0, tiled=True)]
    all_to_all x1 -> x0, blocking collectives: 27.8 us -> none  [per_device(): got = lax.all_to_all(chosen, 'sp', split_axis=0, concat_axis=0, tiled=True)]
    all_to_all x1 -> x0, starting transfers between devices: 10.4 us -> none  [per_device(): lax.all_to_all(asked, 'sp', split_axis=0, concat_axis=0, tiled=True)]
    all_gather x1, blocking collectives: 50.8 us -> 53.2 us  [per_device(): whole = lax.all_gather(sent, 'mem', axis=0, tiled=True)]
  transfers between devices with their start and end apart: 1 -> 0, of which waited for: 0 -> 0; matrix products, arithmetic and copies ran while one was open for 2% -> 0% of each run, Pallas kernels for 0% -> 0%
where the time goes in v4:
time: 96.3 us; the launch traced here: 96.1 us
  blocking collectives  88.9 us (92%)
  matrix products  3.29 us (3%)
  Pallas kernels  1.74 us (2%)
  other arithmetic  1.44 us (1%)
    all_gather x1, blocking collectives, per_device(): whole = lax.all_gather(sent, 'mem', axis=0, tiled=True)  53.2 us
    all_gather x1, blocking collectives, per_device(): every = lax.all_gather(products, 'sp', axis=0, tiled=True)  35.6 us

profile of v4, /device:TPU:1, one launch (start us, length us, event | category | flops | bytes accessed | tf_op | source)
XLA Modules:
  0.0 96.1 jit_solution(10532044803339300687)
XLA Ops:
  0.0 1.0 multiply_convert_fusion
  1.0 53.2 %all-gather.2 = f16[256,6144]{1,0:T(8,128)(2,1)S(1)} all-gather(f16[16,6144]{1,0:T(8,128)(2,1)S(1)} %multiply_convert_fusion), channel_id=1, replica_groups=mesh['mem'=16,'sp'=32] {'mem'}, dimensions={0}, use_global_device_ids=true | all-gather | bytes 3342336 | tf_op jit(solution)/shard_map/all_gather | solution.py:71
  54.2 0.2 convert_reduce_fusion.1
  54.4 1.7 %shard_map.73 = (bf16[16,2048]{1,0:T(8,128)(2,1)}, bf16[32,512]{1,0:T(8,128)(2,1)}) custom-call(bf16[16,2048]{1,0:T(8,128)(2,1)} %predicted_ref.1, f32[1,2048]{1,0:T(1,128)} %bitcast.36, bf16[16,2048]{1,0:T(8,128)(2,1)} %perturbation_ref.1, f32[1,16]{1,0:T(1,128)} %bitcast.37, s32[1,64]{1,0:T(1,128)} %lists_ref.1, s32[32,64]{1,0:T(8,128)} %localization_ref.1), custom_call_target="tpu_custom_call" | custom-call | tf_op jit(solution)/shard_map/pallas_call | solution.py:53
  56.1 0.0 copy-start
  56.1 1.2 %fusion.15 = f16[16,16,256]{2,1,0:T(8,128)(2,1)S(1)} fusion(f32[2048]{0:T(1024)S(1)} %broadcast_multiply_fusion.1, f16[256,6144]{1,0:T(8,128)(2,1)S(1)} %all-gather.2, bf16[16,2048]{1,0:T(8,128)(2,1)} %get-tuple-element.8), kind=kOutput, calls=%fused_computation.17 | convolution fusion | flops 18546688 | bytes 1253376 | tf_op jit(solution)/shard_map/njd,mjd->jnm/dot_general | solution.py:77
  57.3 35.6 %all-gather.3 = f16[512,16,256]{2,1,0:T(8,128)(2,1)S(1)} all-gather(f16[16,16,256]{2,1,0:T(8,128)(2,1)S(1)} %fusion.15), channel_id=1, replica_groups=mesh['mem'=16,'sp'=32] {'sp'}, dimensions={0}, use_global_device_ids=true | all-gather | bytes 4325376 | tf_op jit(solution)/shard_map/all_gather | solution.py:84
  93.0 0.0 copy-done
  93.0 1.5 %fusion.7 = bf16[32,16,256]{2,0,1:T(8,128)(2,1)S(1)} fusion(f16[512,16,256]{2,1,0:T(8,128)(2,1)S(1)} %all-gather.3, bf16[32,512]{1,0:T(8,128)(2,1)S(1)} %copy-done), kind=kOutput, calls=%fused_computation.12 | convolution fusion | flops 136445952 | bytes 4489216 | tf_op jit(solution)/shard_map/bj,jnm->bnm/dot_general | solution.py:85
  94.5 0.3 convert_reduce_fusion
  94.8 0.6 fusion.11
  95.4 0.7 copy.44
  (2 shorter events, 0.0 us)
Async XLA Ops:
  56.1 36.9 %copy-start = (bf16[32,512]{1,0:T(8,128)(2,1)S(1)}, bf16[32,512]{1,0:T(8,128)(2,1)}, u32[]{:S(2)}) copy-start(bf16[32,512]{1,0:T(8,128)(2,1)} %get-tuple-element.7) | copy-start | bytes 98308

commit v5 on v3

--- a/solution.py
+++ b/solution.py
@@ -6,6 +6,7 @@
 from jax.sharding import PartitionSpec as P
 
 SLOTS = 3
+LISTERS = 1
 SCALE = 2.0**13
 
 
@@ -80,14 +81,20 @@
         block_lists,
         localization,
     )
-    wanted = lax.all_to_all(asked, "sp", split_axis=0, concat_axis=0, tiled=True)
-    wanted = wanted[:, :SLOTS].reshape(-1)
-
-    sent = jnp.concatenate([predicted, ensemble], axis=1).astype(f32)
+    wanted = lax.cond(
+        lax.axis_index("mem") == LISTERS,
+        lambda a: lax.all_to_all(a, "sp", split_axis=0, concat_axis=0, tiled=True),
+        lambda a: a,
+        asked,
+    )
+    wanted = wanted[:, :SLOTS].reshape(1, slots).astype(bf16) / blocks
+    wanted = jnp.pad(wanted, ((0, local - 1), (0, -slots % 128)))
+    sent = jnp.concatenate([predicted, ensemble, wanted], axis=1).astype(f32)
     sent = (sent * SCALE).astype(f16)
     whole = lax.all_gather(sent, "mem", axis=0, tiled=True)
     whole_predicted = whole[:, :data].astype(f32)
-    whole_ensemble = whole[:, data:].astype(f32)
+    whole_ensemble = whole[:, data : data + cells].astype(f32)
+    wanted = whole[LISTERS * local, data + cells : data + cells + slots].astype(f32)
 
     data_mean = jnp.sum(whole_predicted, axis=0) / members
     data_anomalies = (whole_predicted - data_mean).astype(bf16)
@@ -97,7 +104,7 @@
         data_anomalies.reshape(members, blocks, block),
         preferred_element_type=f32,
     ).astype(bf16)
-    picked = (wanted[:, None] == jnp.arange(blocks)[None, :]).astype(bf16)
+    picked = (wanted[:, None] == (SCALE / blocks) * jnp.arange(blocks)[None, :]).astype(bf16)
     chosen = jnp.einsum("sj,jnm->snm", picked, products, preferred_element_type=f32).astype(bf16)
     chosen = chosen.reshape(sp, SLOTS * local, members)
     model_mean = jnp.sum(whole_ensemble, axis=0) / members

time: 95.7 us -> 92.9 us (0.971)
  starting transfers between devices: 10.4 us -> 0 us
  blocking collectives: 78.6 us -> 86.2 us
    all_to_all x1 -> x0, starting transfers between devices: 10.4 us -> none  [per_device(): lax.all_to_all(asked, 'sp', split_axis=0, concat_axis=0, tiled=True)]
    all_gather x1, blocking collectives: 50.8 us -> 61 us  [per_device(): whole = lax.all_gather(sent, 'mem', axis=0, tiled=True)]
    all_to_all x1, blocking collectives: 27.8 us -> 25.2 us  [per_device(): got = lax.all_to_all(chosen, 'sp', split_axis=0, concat_axis=0, tiled=True)]
  transfers between devices with their start and end apart: 1 -> 0, of which waited for: 0 -> 0; matrix products, arithmetic and copies ran while one was open for 2% -> 0% of each run, Pallas kernels for 0% -> 0%
where the time goes in v5:
time: 92.9 us; the launch traced here: 92.7 us
  blocking collectives  86.2 us (93%)
  matrix products  1.84 us (2%)
  Pallas kernels  1.82 us (2%)
  other arithmetic  1.45 us (2%)
  local copies, waits for them, and re-layouts  1.29 us (1%)
    all_gather x1, blocking collectives, per_device(): whole = lax.all_gather(sent, 'mem', axis=0, tiled=True)  61 us
    all_to_all x1, blocking collectives, per_device(): got = lax.all_to_all(chosen, 'sp', split_axis=0, concat_axis=0, tiled=True)  25.2 us

profile of v5, /device:TPU:1, one launch (start us, length us, event | category | flops | bytes accessed | tf_op | source)
XLA Modules:
  0.0 92.7 jit_solution(8168053769559570153)
XLA Ops:
  0.0 1.8 %shard_map.73 = (bf16[16,2048]{1,0:T(8,128)(2,1)}, s32[32,128]{1,0:T(8,128)S(1)}, bf16[32,128]{1,0:T(8,128)(2,1)}) custom-call(bf16[16,2048]{1,0:T(8,128)(2,1)} %predicted_ref.1, f32[1,2048]{1,0:T(1,128)} %bitcast.52, bf16[16,2048]{1,0:T(8,128)(2,1)} %perturbation_ref.1, f32[1,16]{1,0:T(1,128)} %bitcast.53, s32[1,64]{1,0:T(1,128)} %lists_ref.1, ...), custom_call_target="tpu_custom_call" | custom-call | tf_op jit(solution)/shard_map/pallas_call | solution.py:67
  1.8 0.1 div.32
  1.9 1.0 %multiply_convert_fusion = f16[16,6272]{1,0:T(8,128)(2,1)S(1)} fusion(bf16[1,96]{1,0:T(2,128)(2,1)S(1)} %div.32, bf16[16,4096]{1,0:T(8,128)(2,1)} %param.9, bf16[16,2048]{1,0:T(8,128)(2,1)} %predicted_ref.1), kind=kLoop, calls=%fused_computation.20 | loop fusion | flops 1003520 | bytes 397504 | tf_op jit(solution)/shard_map/convert_element_type | solution.py:93
  2.9 0.0 copy-start.1
  2.9 61.0 %all-gather.1 = f16[256,6272]{1,0:T(8,128)(2,1)S(1)} all-gather(f16[16,6272]{1,0:T(8,128)(2,1)S(1)} %multiply_convert_fusion), channel_id=1, replica_groups=mesh['mem'=16,'sp'=32] {'mem'}, dimensions={0}, use_global_device_ids=true | all-gather | bytes 3411968 | tf_op jit(solution)/shard_map/all_gather | solution.py:94
  63.9 0.2 convert_reduce_fusion.1
  64.1 0.3 convert_reduce_fusion
  64.4 0.0 copy-start
  64.4 0.0 copy-done.1
  64.4 0.4 convolution_convert_fusion.2
  64.8 0.5 convolution_convert_fusion
  65.3 0.4 copy.22
  65.7 25.2 %all_to_all.15 = bf16[32,48,256]{2,1,0:T(8,128)(2,1)S(1)} all-to-all(bf16[32,48,256]{2,1,0:T(8,128)(2,1)S(1)} %bitcast.48), channel_id=1, replica_groups=mesh['mem'=16,'sp'=32] {'sp'}, dimensions={0} | all-to-all | bytes 1572864 | tf_op jit(solution)/shard_map/all_to_all | solution.py:112
  91.0 0.0 copy-done
  91.0 0.4 convolution_convert_fusion.1
  91.4 0.6 fusion.9
  91.9 0.7 copy.54
  (6 shorter events, 0.0 us)
Async XLA Ops:
  2.9 61.5 %copy-start.1 = (bf16[16,2048]{1,0:T(8,128)(2,1)S(1)}, bf16[16,2048]{1,0:T(8,128)(2,1)}, u32[]{:S(2)}) copy-start(bf16[16,2048]{1,0:T(8,128)(2,1)} %get-tuple-element.23) | copy-start | bytes 196612
  64.4 26.6 %copy-start = (bf16[32,128]{1,0:T(8,128)(2,1)S(1)}, bf16[32,128]{1,0:T(8,128)(2,1)}, u32[]{:S(2)}) copy-start(bf16[32,128]{1,0:T(8,128)(2,1)} %get-tuple-element.26) | copy-start | bytes 24580

commit v6 on v5

--- a/solution.py
+++ b/solution.py
@@ -11,12 +11,15 @@
 
 
 def prepare(
-    predicted_ref, observed_ref, perturbation_ref, variance_ref, lists_ref, localization_ref,
-    weighted_ref, asked_ref, pattern_ref,
+    predicted_ref, ensemble_ref, observed_ref, perturbation_ref, variance_ref, lists_ref, localization_ref,
+    joined_ref, weighted_ref, asked_ref, pattern_ref,
 ):
     bf16, f32 = jnp.bfloat16, jnp.float32
     blocks = variance_ref.shape[1]
-    block = predicted_ref.shape[1] // blocks
+    data = predicted_ref.shape[1]
+    block = data // blocks
+    joined_ref[:, :data] = predicted_ref[...]
+    joined_ref[:, data:] = ensemble_ref[...]
     for j in range(blocks):
         cut = slice(j * block, (j + 1) * block)
         variance = variance_ref[0, j]
@@ -64,17 +67,19 @@
     slots = sp * SLOTS
 
     vmem = pl.BlockSpec(memory_space=pltpu.VMEM)
-    weighted, asked, pattern = pl.pallas_call(
+    joined, weighted, asked, pattern = pl.pallas_call(
         prepare,
         out_shape=(
-            jax.ShapeDtypeStruct((local, data), bf16),
-            jax.ShapeDtypeStruct((sp, 128), jnp.int32),
-            jax.ShapeDtypeStruct((bricks, 128), bf16),
+            pltpu.VMEM((local, data + cells), bf16),
+            pltpu.VMEM((local, data), bf16),
+            pltpu.VMEM((sp, 128), jnp.int32),
+            pltpu.VMEM((bricks, 128), bf16),
         ),
-        in_specs=[vmem, vmem, vmem, pl.BlockSpec(memory_space=pltpu.SMEM), vmem, vmem],
-        out_specs=(vmem, vmem, vmem),
+        in_specs=[vmem, vmem, vmem, vmem, pl.BlockSpec(memory_space=pltpu.SMEM), vmem, vmem],
+        out_specs=(vmem, vmem, vmem, vmem),
     )(
         predicted,
+        ensemble,
         observed.reshape(1, data),
         perturbation,
         noise_variance.reshape(1, blocks),
@@ -89,14 +94,15 @@
     )
     wanted = wanted[:, :SLOTS].reshape(1, slots).astype(bf16) / blocks
     wanted = jnp.pad(wanted, ((0, local - 1), (0, -slots % 128)))
-    sent = jnp.concatenate([predicted, ensemble, wanted], axis=1).astype(f32)
+    sent = jnp.concatenate([joined, wanted], axis=1).astype(f32)
     sent = (sent * SCALE).astype(f16)
     whole = lax.all_gather(sent, "mem", axis=0, tiled=True)
     whole_predicted = whole[:, :data].astype(f32)
     whole_ensemble = whole[:, data : data + cells].astype(f32)
     wanted = whole[LISTERS * local, data + cells : data + cells + slots].astype(f32)
 
-    data_mean = jnp.sum(whole_predicted, axis=0) / members
+    means = jnp.sum(whole.astype(f32), axis=0) / members
+    data_mean, model_mean = means[:data], means[data : data + cells]
     data_anomalies = (whole_predicted - data_mean).astype(bf16)
     products = jnp.einsum(
         "njd,mjd->jnm",
@@ -107,7 +113,6 @@
     picked = (wanted[:, None] == (SCALE / blocks) * jnp.arange(blocks)[None, :]).astype(bf16)
     chosen = jnp.einsum("sj,jnm->snm", picked, products, preferred_element_type=f32).astype(bf16)
     chosen = chosen.reshape(sp, SLOTS * local, members)
-    model_mean = jnp.sum(whole_ensemble, axis=0) / members
     chosen, model_mean, pattern = lax.optimization_barrier((chosen, model_mean, pattern))
     got = lax.all_to_all(chosen, "sp", split_axis=0, concat_axis=0, tiled=True)
     got = got.reshape(slots, local, members)

time: 92.9 us -> 91.3 us (0.983)
  no operation moved by 1% of the time
where the time goes in v6:
time: 91.3 us; the launch traced here: 91.1 us
  blocking collectives  86.1 us (94%)
  matrix products  1.84 us (2%)
  local copies, waits for them, and re-layouts  1.28 us (1%)
  Pallas kernels  1.26 us (1%)
    all_gather x1, blocking collectives, per_device(): whole = lax.all_gather(sent, 'mem', axis=0, tiled=True)  60.8 us
    all_to_all x1, blocking collectives, per_device(): got = lax.all_to_all(chosen, 'sp', split_axis=0, concat_axis=0, tiled=True)  25.2 us

profile of v6, /device:TPU:1, one launch (start us, length us, event | category | flops | bytes accessed | tf_op | source)
XLA Modules:
  0.0 91.1 jit_solution(3892262676621601144)
XLA Ops:
  0.0 1.3 %shard_map.73 = (bf16[16,6144]{1,0:T(8,128)(2,1)S(1)}, bf16[16,2048]{1,0:T(8,128)(2,1)S(1)}, s32[32,128]{1,0:T(8,128)S(1)}, bf16[32,128]{1,0:T(8,128)(2,1)S(1)}) custom-call(bf16[16,2048]{1,0:T(8,128)(2,1)} %predicted_ref.1, bf16[16,4096]{1,0:T(8,128)(2,1)} %ensemble_ref.1, f32[1,2048]{1,0:T(1,128)} %bitcast.52, bf16[16,2048]{1,0:T(8,128)(2,1)} %perturbation_ref.1, ...), custom_call_target="tpu_custom_call" | custom-call | tf_op jit(solution)/shard_map/pallas_call | solution.py:70
  1.3 0.1 div.26
  1.4 0.1 multiply_convert_fusion
  1.5 60.8 %all-gather.1 = f16[256,6272]{1,0:T(8,128)(2,1)S(1)} all-gather(f16[16,6272]{1,0:T(8,128)(2,1)S(1)} %multiply_convert_fusion), channel_id=1, replica_groups=mesh['mem'=16,'sp'=32] {'mem'}, dimensions={0}, use_global_device_ids=true | all-gather | bytes 3411968 | tf_op jit(solution)/shard_map/all_gather | solution.py:99
  62.3 0.5 convert_reduce_fusion
  62.8 0.4 convolution_convert_fusion.2
  63.2 0.5 convolution_convert_fusion
  63.7 0.4 copy.22
  64.1 25.2 %all_to_all.15 = bf16[32,48,256]{2,1,0:T(8,128)(2,1)S(1)} all-to-all(bf16[32,48,256]{2,1,0:T(8,128)(2,1)S(1)} %bitcast.50), channel_id=1, replica_groups=mesh['mem'=16,'sp'=32] {'sp'}, dimensions={0} | all-to-all | bytes 1572864 | tf_op jit(solution)/shard_map/all_to_all | solution.py:117
  89.4 0.4 convolution_convert_fusion.1
  89.8 0.6 fusion.7
  90.3 0.7 copy.54
  (7 shorter events, 0.0 us)

commit v7 on v6

--- a/solution.py
+++ b/solution.py
@@ -6,7 +6,7 @@
 from jax.sharding import PartitionSpec as P
 
 SLOTS = 3
-LISTERS = 1
+LISTERS = 2
 SCALE = 2.0**13
 
 

time: 91.3 us -> 90.7 us (level)
    all_to_all x1, blocking collectives: 25.2 us -> 22.2 us  [per_device(): got = lax.all_to_all(chosen, 'sp', split_axis=0, concat_axis=0, tiled=True)]
    all_gather x1, blocking collectives: 60.8 us -> 63.3 us  [per_device(): whole = lax.all_gather(sent, 'mem', axis=0, tiled=True)]
where the time goes in v7:
time: 90.7 us; the launch traced here: 90.5 us
  blocking collectives  85.5 us (94%)
  matrix products  1.84 us (2%)
  local copies, waits for them, and re-layouts  1.28 us (1%)
  Pallas kernels  1.26 us (1%)
    all_gather x1, blocking collectives, per_device(): whole = lax.all_gather(sent, 'mem', axis=0, tiled=True)  63.3 us
    all_to_all x1, blocking collectives, per_device(): got = lax.all_to_all(chosen, 'sp', split_axis=0, concat_axis=0, tiled=True)  22.2 us

profile of v7, /device:TPU:1, one launch (start us, length us, event | category | flops | bytes accessed | tf_op | source)
XLA Modules:
  0.0 90.5 jit_solution(9501471484145851451)
XLA Ops:
  0.0 1.3 %shard_map.73 = (bf16[16,6144]{1,0:T(8,128)(2,1)S(1)}, bf16[16,2048]{1,0:T(8,128)(2,1)S(1)}, s32[32,128]{1,0:T(8,128)S(1)}, bf16[32,128]{1,0:T(8,128)(2,1)S(1)}) custom-call(bf16[16,2048]{1,0:T(8,128)(2,1)} %predicted_ref.1, bf16[16,4096]{1,0:T(8,128)(2,1)} %ensemble_ref.1, f32[1,2048]{1,0:T(1,128)} %bitcast.52, bf16[16,2048]{1,0:T(8,128)(2,1)} %perturbation_ref.1, ...), custom_call_target="tpu_custom_call" | custom-call | tf_op jit(solution)/shard_map/pallas_call | solution.py:70
  1.3 0.1 div.26
  1.4 0.1 multiply_convert_fusion
  1.5 63.3 %all-gather.1 = f16[256,6272]{1,0:T(8,128)(2,1)S(1)} all-gather(f16[16,6272]{1,0:T(8,128)(2,1)S(1)} %multiply_convert_fusion), channel_id=1, replica_groups=mesh['mem'=16,'sp'=32] {'mem'}, dimensions={0}, use_global_device_ids=true | all-gather | bytes 3411968 | tf_op jit(solution)/shard_map/all_gather | solution.py:99
  64.7 0.5 convert_reduce_fusion
  65.2 0.4 convolution_convert_fusion.2
  65.6 0.5 convolution_convert_fusion
  66.1 0.4 copy.22
  66.5 22.2 %all_to_all.15 = bf16[32,48,256]{2,1,0:T(8,128)(2,1)S(1)} all-to-all(bf16[32,48,256]{2,1,0:T(8,128)(2,1)S(1)} %bitcast.50), channel_id=1, replica_groups=mesh['mem'=16,'sp'=32] {'sp'}, dimensions={0} | all-to-all | bytes 1572864 | tf_op jit(solution)/shard_map/all_to_all | solution.py:117
  88.8 0.4 convolution_convert_fusion.1
  89.2 0.6 fusion.7
  89.8 0.7 copy.54
  (7 shorter events, 0.0 us)

commit v8 on v7

--- a/solution.py
+++ b/solution.py
@@ -6,7 +6,6 @@
 from jax.sharding import PartitionSpec as P
 
 SLOTS = 3
-LISTERS = 2
 SCALE = 2.0**13
 
 
@@ -86,9 +85,14 @@
         block_lists,
         localization,
     )
+    groups = [[m * sp + t for t in range(sp)] for m in range(mem)]
+    groups[0][0], groups[1][0] = groups[1][0], groups[0][0]
+    lister = (lax.axis_index("sp") == 0).astype(jnp.int32)
     wanted = lax.cond(
-        lax.axis_index("mem") == LISTERS,
-        lambda a: lax.all_to_all(a, "sp", split_axis=0, concat_axis=0, tiled=True),
+        lax.axis_index("mem") == lister,
+        lambda a: lax.all_to_all(
+            a, ("mem", "sp"), split_axis=0, concat_axis=0, tiled=True, axis_index_groups=groups
+        ),
         lambda a: a,
         asked,
     )
@@ -99,7 +103,8 @@
     whole = lax.all_gather(sent, "mem", axis=0, tiled=True)
     whole_predicted = whole[:, :data].astype(f32)
     whole_ensemble = whole[:, data : data + cells].astype(f32)
-    wanted = whole[LISTERS * local, data + cells : data + cells + slots].astype(f32)
+    tables = whole[:, data + cells : data + cells + slots]
+    wanted = jnp.where(lister == 1, tables[local], tables[0]).astype(f32)
 
     means = jnp.sum(whole.astype(f32), axis=0) / members
     data_mean, model_mean = means[:data], means[data : data + cells]

time: 90.7 us -> 91 us (level)
    all_gather x1, blocking collectives: 63.3 us -> 45 us  [per_device(): whole = lax.all_gather(sent, 'mem', axis=0, tiled=True)]
    all_to_all x0 -> x1, blocking collectives: none -> 16.2 us  [per_device(): lax.all_to_all(a, ('mem', 'sp'), split_axis=0, concat_axis=0, tiled=True,...]
    all_to_all x1, blocking collectives: 22.2 us -> 24.6 us  [per_device(): got = lax.all_to_all(chosen, 'sp', split_axis=0, concat_axis=0, tiled=True)]
where the time goes in v8:
time: 91 us; the launch traced here: 90.8 us
  blocking collectives  85.8 us (94%)
  matrix products  1.84 us (2%)
  local copies, waits for them, and re-layouts  1.29 us (1%)
  Pallas kernels  1.26 us (1%)
    all_gather x1, blocking collectives, per_device(): whole = lax.all_gather(sent, 'mem', axis=0, tiled=True)  45 us
    all_to_all x1, blocking collectives, per_device(): got = lax.all_to_all(chosen, 'sp', split_axis=0, concat_axis=0, tiled=True)  24.6 us
    all_to_all x1, blocking collectives, per_device(): lax.all_to_all(a, ('mem', 'sp'), split_axis=0, concat_axis=0, tiled=True,...  16.2 us

profile of v8, /device:TPU:1, one launch (start us, length us, event | category | flops | bytes accessed | tf_op | source)
XLA Modules:
  0.0 90.8 jit_solution(6800064558899071463)
XLA Ops:
  0.0 1.3 %shard_map.73 = (bf16[16,6144]{1,0:T(8,128)(2,1)S(1)}, bf16[16,2048]{1,0:T(8,128)(2,1)S(1)}, s32[32,128]{1,0:T(8,128)S(1)}, bf16[32,128]{1,0:T(8,128)(2,1)S(1)}) custom-call(bf16[16,2048]{1,0:T(8,128)(2,1)} %predicted_ref.1, bf16[16,4096]{1,0:T(8,128)(2,1)} %ensemble_ref.1, f32[1,2048]{1,0:T(1,128)} %bitcast.52, bf16[16,2048]{1,0:T(8,128)(2,1)} %perturbation_ref.1, ...), custom_call_target="tpu_custom_call" | custom-call | tf_op jit(solution)/shard_map/pallas_call | solution.py:69
  1.3 16.2 %conditional.1 = (s32[32,128]{1,0:T(8,128)S(1)}) conditional(s32[]{:T(128)} %convert_element_type.78, s32[32,128]{1,0:T(8,128)S(1)} %get-tuple-element.24, s32[32,128]{1,0:T(8,128)S(1)} %get-tuple-element.24), branch_computations={%region_0.0_spmd, %region_1.0_spmd} | conditional | bytes 65544 | solution.py:91
  1.3 16.2 %all_to_all.14 = s32[32,1,128]{2,1,0:T(1,128)S(1)} all-to-all(s32[32,1,128]{2,1,0:T(1,128)S(1)} %copy.57), channel_id=1, replica_groups={{32,1,2,3,4,5,6,7,8,9,10,11,12,13,14,15,16,17,18,19,20,21,22,23,24,25,2..., dimensions={0} | all-to-all | bytes 32768 | tf_op jit(solution)/shard_map/cond/branch_1_fun/all_to_all | solution.py:93
  17.5 0.1 div.26
  17.6 0.1 multiply_convert_fusion
  17.7 45.0 %all-gather.1 = f16[256,6272]{1,0:T(8,128)(2,1)S(1)} all-gather(f16[16,6272]{1,0:T(8,128)(2,1)S(1)} %multiply_convert_fusion), channel_id=1, replica_groups=mesh['mem'=16,'sp'=32] {'mem'}, dimensions={0}, use_global_device_ids=true | all-gather | bytes 3411968 | tf_op jit(solution)/shard_map/all_gather | solution.py:103
  62.7 0.5 convert_reduce_fusion
  63.2 0.4 convolution_convert_fusion.2
  63.6 0.5 convolution_convert_fusion
  64.1 0.4 copy.22
  64.5 24.6 %all_to_all.15 = bf16[32,48,256]{2,1,0:T(8,128)(2,1)S(1)} all-to-all(bf16[32,48,256]{2,1,0:T(8,128)(2,1)S(1)} %bitcast.50), channel_id=1, replica_groups=mesh['mem'=16,'sp'=32] {'sp'}, dimensions={0} | all-to-all | bytes 1572864 | tf_op jit(solution)/shard_map/all_to_all | solution.py:122
  89.1 0.4 convolution_convert_fusion.1
  89.5 0.6 fusion.7
  90.1 0.7 copy.54
  (7 shorter events, 0.0 us)

commit v9 on v7

--- a/solution.py
+++ b/solution.py
@@ -101,8 +101,8 @@
     whole_ensemble = whole[:, data : data + cells].astype(f32)
     wanted = whole[LISTERS * local, data + cells : data + cells + slots].astype(f32)
 
-    means = jnp.sum(whole.astype(f32), axis=0) / members
-    data_mean, model_mean = means[:data], means[data : data + cells]
+    data_mean = jnp.sum(whole_predicted, axis=0) / members
+    model_mean = jnp.sum(whole_ensemble, axis=0) / members
     data_anomalies = (whole_predicted - data_mean).astype(bf16)
     products = jnp.einsum(
         "njd,mjd->jnm",

time: 90.7 us -> 90.7 us (level)
  no operation moved by 1% of the time
where the time goes in v9:
time: 90.7 us; the launch traced here: 90.5 us
  blocking collectives  85.5 us (94%)
  matrix products  1.83 us (2%)
  local copies, waits for them, and re-layouts  1.28 us (1%)
  Pallas kernels  1.26 us (1%)
    all_gather x1, blocking collectives, per_device(): whole = lax.all_gather(sent, 'mem', axis=0, tiled=True)  63.3 us
    all_to_all x1, blocking collectives, per_device(): got = lax.all_to_all(chosen, 'sp', split_axis=0, concat_axis=0, tiled=True)  22.2 us

profile of v9, /device:TPU:1, one launch (start us, length us, event | category | flops | bytes accessed | tf_op | source)
XLA Modules:
  0.0 90.5 jit_solution(8139647293344957874)
XLA Ops:
  0.0 1.3 %shard_map.73 = (bf16[16,6144]{1,0:T(8,128)(2,1)S(1)}, bf16[16,2048]{1,0:T(8,128)(2,1)S(1)}, s32[32,128]{1,0:T(8,128)S(1)}, bf16[32,128]{1,0:T(8,128)(2,1)S(1)}) custom-call(bf16[16,2048]{1,0:T(8,128)(2,1)} %predicted_ref.1, bf16[16,4096]{1,0:T(8,128)(2,1)} %ensemble_ref.1, f32[1,2048]{1,0:T(1,128)} %bitcast.52, bf16[16,2048]{1,0:T(8,128)(2,1)} %perturbation_ref.1, ...), custom_call_target="tpu_custom_call" | custom-call | tf_op jit(solution)/shard_map/pallas_call | solution.py:70
  1.3 0.1 div.32
  1.4 0.1 multiply_convert_fusion
  1.5 63.3 %all-gather.1 = f16[256,6272]{1,0:T(8,128)(2,1)S(1)} all-gather(f16[16,6272]{1,0:T(8,128)(2,1)S(1)} %multiply_convert_fusion), channel_id=1, replica_groups=mesh['mem'=16,'sp'=32] {'mem'}, dimensions={0}, use_global_device_ids=true | all-gather | bytes 3411968 | tf_op jit(solution)/shard_map/all_gather | solution.py:99
  64.7 0.2 convert_reduce_fusion.1
  64.9 0.3 convert_reduce_fusion
  65.2 0.4 convolution_convert_fusion.2
  65.6 0.5 convolution_convert_fusion
  66.1 0.4 copy.22
  66.5 22.2 %all_to_all.15 = bf16[32,48,256]{2,1,0:T(8,128)(2,1)S(1)} all-to-all(bf16[32,48,256]{2,1,0:T(8,128)(2,1)S(1)} %bitcast.50), channel_id=1, replica_groups=mesh['mem'=16,'sp'=32] {'sp'}, dimensions={0} | all-to-all | bytes 1572864 | tf_op jit(solution)/shard_map/all_to_all | solution.py:117
  88.8 0.4 convolution_convert_fusion.1
  89.2 0.6 fusion.9
  89.7 0.7 copy.54
  (6 shorter events, 0.0 us)
